TPU v7x, 512 devices: a whole 4x4x16 slice. The times are simulated.
512 devices in a mesh: dp: 32 (over z, x_hi), mp: 16 (over x_lo, y, core).
Axes of the slice: x: 4 (x_hi: 2, x_lo: 2; x = x_hi * 2 + x_lo), y: 4, z: 16, core: 2. Of those that a mesh axis runs over, the one named last changes fastest.
Arguments:
- tokens: bfloat16 [32768, 2048], P('dp', 'mp'), may hold values from -6 to 6
- norm_gain: bfloat16 [2048], replicated, may hold values from 0.099609375 to 1.8984375
- wi_gate: bfloat16 [2048, 5120], P(None, 'mp'), may hold values from -0.125 to 0.125
- wi_linear: bfloat16 [2048, 5120], P(None, 'mp'), may hold values from -0.125 to 0.125
- wo_out: bfloat16 [5120, 2048], P('mp'), may hold values from -0.078125 to 0.078125
- task_table: float32 [8, 64], replicated, may hold values from -5 to 5
- layer_table: float32 [24, 64], replicated, may hold values from -5 to 5
- task_ids: int32 [256], P('dp'), may hold values from 0 to 7
- layer_index: int32 [1], replicated, may hold values from 0 to 23
- hyper_in: bfloat16 [128, 1024], P(None, 'mp'), may hold values from -0.5 to 0.5
- gen_down: bfloat16 [1024, 131072], P(None, ('mp', 'dp')), may hold values from -0.0078125 to 0.0078125
- gen_up: bfloat16 [1024, 131072], P(None, ('mp', 'dp')), may hold values from -0.046875 to 0.046875
Outputs:
- mixed: bfloat16 [32768, 2048], P('dp', 'mp')
All inputs are finite; a program needn't handle non-finite values.
Results may differ from a plain program's by a relative error of at most 0.019.
Values may be sent and summed in bfloat16 or wider, within the bound.
No kernel may reach another device: no remote copies, remote signals or barrier semaphores. Data moves between devices by JAX's collectives and lax.ppermute only.
A program may use at most 64 MiB of HBM per device.

v0:
```python
import jax
import jax.numpy as jnp
from jax import lax
from jax.sharding import PartitionSpec as P

R = 64


def laid_out(blocks, dim):
    lengths = list(blocks.shape[1:])
    lengths[dim] *= blocks.shape[0]
    return jnp.moveaxis(blocks, 0, dim).reshape(lengths)


def from_everyone(shard, axis):
    copies = jnp.broadcast_to(shard, (lax.axis_size(axis), *shard.shape))
    return lax.all_to_all(copies, axis, split_axis=0, concat_axis=0, tiled=True)


def gather_directly(shard, axis, dim):
    return laid_out(from_everyone(shard, axis), dim)


def of_everyone(shard, axis):
    everything = from_everyone(shard, axis)
    return jnp.sum(everything.astype(jnp.float32), axis=0)


def matmul(left, right):
    return jnp.dot(left, right, preferred_element_type=jnp.float32)


def per_device(
    tokens,
    norm_gain,
    wi_gate,
    wi_linear,
    wo_out,
    task_table,
    layer_table,
    task_ids,
    layer_index,
    hyper_in,
    gen_down,
    gen_up,
):
    task_count = task_table.shape[0]
    layer_row = jnp.take(layer_table, layer_index, axis=0)
    embed = jnp.concatenate(
        [task_table, jnp.broadcast_to(layer_row, (task_count, layer_row.shape[1]))], axis=1
    ).astype(jnp.bfloat16)
    hidden_part = jnp.maximum(matmul(embed, hyper_in), 0.0).astype(jnp.bfloat16)
    hidden = gather_directly(hidden_part, "mp", 1)
    every_id = gather_directly(task_ids, "dp", 0)
    wanted = jnp.take(hidden, every_id, axis=0)
    made = (
        matmul(wanted, gen_down).astype(jnp.bfloat16),
        matmul(wanted, gen_up).astype(jnp.bfloat16),
    )
    local_down, local_up = (
        lax.all_to_all(made[0], "dp", split_axis=0, concat_axis=1, tiled=True),
        lax.all_to_all(made[1], "dp", split_axis=0, concat_axis=1, tiled=True),
    )
    full_rows = lax.all_gather(tokens, "mp", axis=1, tiled=True)
    wide = full_rows.astype(jnp.float32)
    scale = lax.rsqrt(jnp.mean(wide * wide, axis=-1, keepdims=True) + 1e-06)
    normed = (wide * scale * norm_gain.astype(jnp.float32)).astype(jnp.bfloat16)
    gate = matmul(normed, wi_gate)
    linear = matmul(normed, wi_linear)
    act = (jax.nn.gelu(gate, approximate=True) * linear).astype(jnp.bfloat16)
    seqs_dev = task_ids.shape[0]
    tok_dev = tokens.shape[0]
    seq_len = tok_dev // seqs_dev
    partial_sums = matmul(act, wo_out)
    ffout = lax.psum_scatter(
        partial_sums.astype(jnp.bfloat16), "mp", scatter_dimension=1, tiled=True
    )
    down_block = local_down.reshape(seqs_dev, -1, R)
    up_block = local_up.reshape(seqs_dev, -1, R)
    blocks = ffout.reshape(seqs_dev, seq_len, -1)
    squeeze_part = jnp.einsum(
        "std,sdr->str", blocks, down_block, preferred_element_type=jnp.float32
    )
    squeeze_full = of_everyone(squeeze_part.astype(jnp.bfloat16), "mp").astype(jnp.float32)
    squeezed = jnp.maximum(squeeze_full, 0.0).astype(jnp.bfloat16)
    expand = jnp.einsum("str,sdr->std", squeezed, up_block, preferred_element_type=jnp.float32)
    total = tokens.astype(jnp.float32) + ffout.astype(jnp.float32) + expand.reshape(tok_dev, -1)
    return total.astype(jnp.bfloat16)


def solution(mesh):
    return jax.shard_map(
        per_device,
        mesh=mesh,
        in_specs=(
            P("dp", "mp"),
            P(),
            P(None, "mp"),
            P(None, "mp"),
            P("mp", None),
            P(),
            P(),
            P("dp"),
            P(),
            P(None, "mp"),
            P(None, ("mp", "dp")),
            P(None, ("mp", "dp")),
        ),
        out_specs=P("dp", "mp"),
        check_vma=False,
    )
```

profile of v0, /device:TPU:25, one launch (start us, length us, event | category | flops | bytes accessed | tf_op | source)
XLA Modules:
  0.0 219.2 jit_solution(13709303609028139173)
XLA Ops:
  6.5 0.7 all-gather.2.cloned.1.call-update
  7.3 0.7 convert_element_type.45
  8.0 58.1 %all-gather.2.cloned.1.call-done = bf16[1024,2048]{1,0:T(8,128)(2,1)} async-done(((bf16[1024,128]{1,0:T(8,128)(2,1)}), bf16[1024,2048]{1,0:T(8,128)(2,1)}) %all-gather.2.cloned.1.call-update) | async-done | bytes 4194320 | tf_op jit(solution)/shard_map/all_gather | solution.py:64
  66.1 3.2 %fusion = f32[1024]{0:T(1024)S(1)} fusion(bf16[1024,2048]{1,0:T(8,128)(2,1)} %all-gather.2.cloned.1.call-done), kind=kLoop, calls=%fused_computation.3 | loop fusion | flops 6290432 | bytes 4198400 | tf_op jit(solution)/shard_map/reduce_sum | solution.py:66
  69.5 4.2 %fusion.12 = f32[1024,320]{0,1:T(8,128)} fusion(bf16[2048,320]{0,1:T(8,128)(2,1)} %param.14, bf16[1024,2048]{1,0:T(8,128)(2,1)S(1)} %copy-done.1, f32[2048]{0:T(1024)S(1)} %convert_element_type.45, f32[1024]{0:T(1024)S(1)} %add_rsqrt_fusion), kind=kOutput, calls=%fused_computation.18 | convolution fusion | flops 1350565888 | bytes 6828032 | tf_op jit(solution)/shard_map/dot_general | solution.py:30
  73.8 8.6 %convolution_convert_fusion = bf16[1024,2048]{1,0:T(8,128)(2,1)} fusion(bf16[320,2048]{1,0:T(8,128)(2,1)S(1)} %copy-done, bf16[2048,320]{0,1:T(8,128)(2,1)S(1)} %copy-done.10, f32[1024,320]{0,1:T(8,128)} %fusion.12, bf16[1024,2048]{1,0:T(8,128)(2,1)} %all-gather.2.cloned.1.call-done, f32[2048]{0:T(1024)S(1)} %convert_element_type.45, f32[1024]{0:T(1024)S(1)} %add_rsqrt_fusion), kind=kOutput, calls=%fused_computation.7 | convolution fusion | flops 2698117120 | bytes 12333056 | tf_op jit(solution)/shard_map/dot_general | solution.py:30
  82.4 6.4 %copy.23 = bf16[1024,2048]{0,1:T(8,128)(2,1)} copy(bf16[1024,2048]{1,0:T(8,128)(2,1)} %convolution_convert_fusion) | data formatting | bytes 8388608
  88.8 0.6 copy-done.9
  89.4 0.6 broadcast_in_dim.38
  90.0 14.2 %all-to-all-start = ((s32[32,1,8]{2,1,0:T(1,128)}), s32[32,1,8]{2,1,0:T(1,128)S(1)}, u32[]{:S(2)}, u32[]{:S(2)}) async-start(s32[32,1,8]{2,1,0:T(1,128)} %broadcast_in_dim.38), calls=%async_computation | async-start | bytes 32768 | tf_op jit(solution)/shard_map/all_to_all | solution.py:17
  105.0 0.7 fusion.30
  105.9 0.7 reshape.145
  106.6 11.3 %all-to-all-done = s32[32,1,8]{2,1,0:T(1,128)S(1)} async-done(((s32[32,1,8]{2,1,0:T(1,128)}), s32[32,1,8]{2,1,0:T(1,128)S(1)}, u32[]{:S(2)}, u32[]{:S(2)}) %all-to-all-start) | async-done | bytes 1056 | tf_op jit(solution)/shard_map/all_to_all | solution.py:17
  117.9 6.1 %all-to-all-start.1 = ((bf16[16,2,256]{2,1,0:T(2,128)(2,1)}), bf16[16,2,256]{2,1,0:T(2,128)(2,1)S(1)}, u32[]{:S(2)}, u32[]{:S(2)}) async-start(bf16[16,2,256]{2,1,0:T(2,128)(2,1)} %reshape.145), calls=%async_computation.1 | async-start | bytes 32768 | tf_op jit(solution)/shard_map/all_to_all | solution.py:17
  124.7 0.7 reduce.5
  125.6 2.6 %all-to-all-done.1 = bf16[16,2,256]{2,1,0:T(2,128)(2,1)S(1)} async-done(((bf16[16,2,256]{2,1,0:T(2,128)(2,1)}), bf16[16,2,256]{2,1,0:T(2,128)(2,1)S(1)}, u32[]{:S(2)}, u32[]{:S(2)}) %all-to-all-start.1) | async-done | bytes 16416 | tf_op jit(solution)/shard_map/all_to_all | solution.py:17
  128.4 1.2 gather_fusion
  129.6 1.0 fusion.14
  130.6 3.8 %all-to-all-start.2 = ((bf16[32,8,256]{2,1,0:T(8,128)(2,1)}), bf16[32,8,256]{2,1,0:T(8,128)(2,1)S(1)}, u32[]{:S(2)}, u32[]{:S(2)}) async-start(bf16[32,8,256]{2,1,0:T(8,128)(2,1)} %fusion.14), calls=%async_computation.2 | async-start | bytes 262144 | tf_op jit(solution)/shard_map/all_to_all | solution.py:61
  134.4 1.0 fusion.15
  135.4 14.6 %all-to-all-done.2 = bf16[32,8,256]{2,1,0:T(8,128)(2,1)S(1)} async-done(((bf16[32,8,256]{2,1,0:T(8,128)(2,1)}), bf16[32,8,256]{2,1,0:T(8,128)(2,1)S(1)}, u32[]{:S(2)}, u32[]{:S(2)}) %all-to-all-start.2) | async-done | bytes 131104 | tf_op jit(solution)/shard_map/all_to_all | solution.py:61
  150.0 5.2 %all-to-all-start.4 = ((bf16[32,8,256]{2,1,0:T(8,128)(2,1)}), bf16[32,8,256]{2,1,0:T(8,128)(2,1)S(1)}, u32[]{:S(2)}, u32[]{:S(2)}) async-start(bf16[32,8,256]{2,1,0:T(8,128)(2,1)} %fusion.15), calls=%async_computation.4 | async-start | bytes 262144 | tf_op jit(solution)/shard_map/all_to_all | solution.py:62
  155.4 7.9 %reduce-scatter.4.cloned.1.call-done = bf16[128,1024]{1,0:T(8,128)(2,1)} async-done(((bf16[2048,1024]{1,0:T(8,128)(2,1)}), bf16[128,1024]{1,0:T(8,128)(2,1)}) %reduce-scatter.4.cloned.1.call-update) | async-done | bytes 262160
  163.4 1.1 copy.24
  164.8 5.2 %all-to-all-done.4 = bf16[32,8,256]{2,1,0:T(8,128)(2,1)S(1)} async-done(((bf16[32,8,256]{2,1,0:T(8,128)(2,1)}), bf16[32,8,256]{2,1,0:T(8,128)(2,1)S(1)}, u32[]{:S(2)}, u32[]{:S(2)}) %all-to-all-start.4) | async-done | bytes 131104 | tf_op jit(solution)/shard_map/all_to_all | solution.py:62
  170.0 1.9 broadcast_in_dim.46
  171.9 8.9 %all-to-all-start.3 = ((bf16[16,8,128,64]{2,3,1,0:T(8,128)(2,1)}), bf16[16,8,128,64]{2,3,1,0:T(8,128)(2,1)S(1)}, u32[]{:S(2)}, u32[]{:S(2)}) async-start(bf16[16,8,128,64]{2,3,1,0:T(8,128)(2,1)} %broadcast_in_dim.46), calls=%async_computation.3 | async-start | bytes 4194304 | tf_op jit(solution)/shard_map/all_to_all | solution.py:17
  180.8 0.9 copy.19
  181.7 0.9 reshape.93
  182.6 27.8 %all-to-all-done.3 = bf16[16,8,128,64]{2,3,1,0:T(8,128)(2,1)S(1)} async-done(((bf16[16,8,128,64]{2,3,1,0:T(8,128)(2,1)}), bf16[16,8,128,64]{2,3,1,0:T(8,128)(2,1)S(1)}, u32[]{:S(2)}, u32[]{:S(2)}) %all-to-all-start.3) | async-done | bytes 2097184 | tf_op jit(solution)/shard_map/all_to_all | solution.py:17
  210.7 0.6 copy-done.5
  211.6 0.8 fusion.23
  (46 shorter events, 2.6 us)
Async XLA Ops:
  6.5 67.2 %copy-start = (bf16[320,2048]{1,0:T(8,128)(2,1)S(1)}, bf16[320,2048]{1,0:T(8,128)(2,1)}, u32[]{:S(2)}) copy-start(bf16[320,2048]{1,0:T(8,128)(2,1)} %param.16) | copy-start | bytes 3932164
  6.5 59.6 %all-gather.2.cloned.1.call-start = ((), (), s32[]{:S(2)}) async-start(), calls=%async_computation.6 | async-start | bytes 4456448 | tf_op jit(solution)/shard_map/all_gather | solution.py:64
  7.3 156.1 %reduce-scatter.4.cloned.1.call-start = ((), (), s32[]{:S(2)}) async-start(), calls=%async_computation.7 | async-start | bytes 4456448
  66.1 3.4 %copy-start.1 = (bf16[1024,2048]{1,0:T(8,128)(2,1)S(1)}, bf16[1024,2048]{1,0:T(8,128)(2,1)}, u32[]{:S(2)}) copy-start(bf16[1024,2048]{1,0:T(8,128)(2,1)} %all-gather.2.cloned.1.call-done) | copy-start | bytes 12582916
  69.5 4.2 %copy-start.10 = (bf16[2048,320]{0,1:T(8,128)(2,1)S(1)}, bf16[2048,320]{0,1:T(8,128)(2,1)}, u32[]{:S(2)}) copy-start(bf16[2048,320]{0,1:T(8,128)(2,1)} %param.15) | copy-start | bytes 3932164
  88.8 0.7 copy-start.9
  88.8 16.2 %copy-start.8 = (f32[8,64]{1,0:T(8,128)S(1)}, f32[8,64]{1,0:T(8,128)}, u32[]{:S(2)}) copy-start(f32[8,64]{1,0:T(8,128)} %param.17) | copy-start | bytes 6148
  88.8 17.0 %copy-start.7 = (bf16[128,64]{0,1:T(8,128)(2,1)S(1)}, bf16[128,64]{0,1:T(8,128)(2,1)}, u32[]{:S(2)}) copy-start(bf16[128,64]{0,1:T(8,128)(2,1)} %param.21) | copy-start | bytes 49156
  90.0 27.9 %all-to-all-start = ((s32[32,1,8]{2,1,0:T(1,128)}), s32[32,1,8]{2,1,0:T(1,128)S(1)}, u32[]{:S(2)}, u32[]{:S(2)}) async-start(s32[32,1,8]{2,1,0:T(1,128)} %broadcast_in_dim.38), calls=%async_computation | async-start | bytes 32768 | tf_op jit(solution)/shard_map/all_to_all | solution.py:17
  117.9 10.2 %all-to-all-start.1 = ((bf16[16,2,256]{2,1,0:T(2,128)(2,1)}), bf16[16,2,256]{2,1,0:T(2,128)(2,1)S(1)}, u32[]{:S(2)}, u32[]{:S(2)}) async-start(bf16[16,2,256]{2,1,0:T(2,128)(2,1)} %reshape.145), calls=%async_computation.1 | async-start | bytes 32768 | tf_op jit(solution)/shard_map/all_to_all | solution.py:17
  128.4 1.2 copy-start.11
  129.6 4.9 %copy-start.12 = (bf16[1024,256]{1,0:T(8,128)(2,1)S(1)}, bf16[1024,256]{1,0:T(8,128)(2,1)}, u32[]{:S(2)}) copy-start(bf16[1024,256]{1,0:T(8,128)(2,1)} %param.23) | copy-start | bytes 1572868
  130.6 19.4 %all-to-all-start.2 = ((bf16[32,8,256]{2,1,0:T(8,128)(2,1)}), bf16[32,8,256]{2,1,0:T(8,128)(2,1)S(1)}, u32[]{:S(2)}, u32[]{:S(2)}) async-start(bf16[32,8,256]{2,1,0:T(8,128)(2,1)} %fusion.14), calls=%async_computation.2 | async-start | bytes 262144 | tf_op jit(solution)/shard_map/all_to_all | solution.py:61
  150.0 20.0 %all-to-all-start.4 = ((bf16[32,8,256]{2,1,0:T(8,128)(2,1)}), bf16[32,8,256]{2,1,0:T(8,128)(2,1)S(1)}, u32[]{:S(2)}, u32[]{:S(2)}) async-start(bf16[32,8,256]{2,1,0:T(8,128)(2,1)} %fusion.15), calls=%async_computation.4 | async-start | bytes 262144 | tf_op jit(solution)/shard_map/all_to_all | solution.py:62
  164.5 7.4 %copy-start.2 = (bf16[1024,128]{1,0:T(8,128)(2,1)}, bf16[1024,128]{1,0:T(8,128)(2,1)S(1)}, u32[]{:S(2)}) copy-start(bf16[1024,128]{1,0:T(8,128)(2,1)S(1)} %copy.24) | copy-start | bytes 786436
  170.0 1.9 copy-start.6
  171.9 38.4 %all-to-all-start.3 = ((bf16[16,8,128,64]{2,3,1,0:T(8,128)(2,1)}), bf16[16,8,128,64]{2,3,1,0:T(8,128)(2,1)S(1)}, u32[]{:S(2)}, u32[]{:S(2)}) async-start(bf16[16,8,128,64]{2,3,1,0:T(8,128)(2,1)} %broadcast_in_dim.46), calls=%async_computation.3 | async-start | bytes 4194304 | tf_op jit(solution)/shard_map/all_to_all | solution.py:17
  210.3 1.0 copy-start.5
  210.3 1.3 copy-start.3
  210.3 1.3 copy-start.4
Sparse Core Ops, SparseCore 0:
  9.4 56.6 all-gather.1
  88.9 74.3 reduce-scatter.3
where the time goes:
time: 220 us; the launch traced here: 219 us
  waiting for transfers between devices  128 us (58%)
  starting transfers between devices  38.3 us (17%)
  local copies, waits for them, and re-layouts  16.4 us (7%)
  matrix products  15.6 us (7%)
  between operations  14.2 us (6%)
  other arithmetic  6.5 us (3%)
    all_gather x1, waiting for transfers between devices, per_device(): full_rows = lax.all_gather(tokens, 'mp', axis=1, tiled=True)  58.1 us
    all_to_all x3, waiting for transfers between devices, from_everyone(): return lax.all_to_all(copies, axis, split_axis=0, concat_axis=0, tiled=True)  41.7 us
    all_to_all x3, starting transfers between devices, from_everyone(): return lax.all_to_all(copies, axis, split_axis=0, concat_axis=0, tiled=True)  29.2 us
    dot_general x5, matrix products, matmul(): return jnp.dot(left, right, preferred_element_type=jnp.float32)  15 us
    all_to_all x1, waiting for transfers between devices, per_device(): lax.all_to_all(made[0], 'dp', split_axis=0, concat_axis=1, tiled=True)  14.6 us
    unnamed x30, local copies, waits for them, and re-layouts  9.83 us
    unnamed x3, waiting for transfers between devices  8.67 us
    all_to_all x1, starting transfers between devices, per_device(): lax.all_to_all(made[1], 'dp', split_axis=0, concat_axis=1, tiled=True)  5.21 us
  transfers between devices with their start and end apart: 7, of which 7 were waited for; matrix products, arithmetic and copies ran while one was open for 5% of the time, Pallas kernels for 0%

commit v1 on v0

--- a/solution.py
+++ b/solution.py
@@ -4,6 +4,12 @@
 from jax.sharding import PartitionSpec as P
 
 R = 64
+
+
+def swap_blocks(x, axis, split, join):
+    parts = jnp.split(x, lax.axis_size(axis), axis=split)
+    received = lax.all_to_all(jnp.stack(parts), axis, 0, 0)
+    return jnp.concatenate(received, axis=join)
 
 
 def laid_out(blocks, dim):
@@ -59,7 +65,7 @@
     )
     local_down, local_up = (
         lax.all_to_all(made[0], "dp", split_axis=0, concat_axis=1, tiled=True),
-        lax.all_to_all(made[1], "dp", split_axis=0, concat_axis=1, tiled=True),
+        swap_blocks(made[1], "dp", 0, 1),
     )
     full_rows = lax.all_gather(tokens, "mp", axis=1, tiled=True)
     wide = full_rows.astype(jnp.float32)

time: 220 us -> 213 us (0.968)
  waiting for transfers between devices: 128 us -> 81.4 us
  starting transfers between devices: 38.3 us -> 58.5 us
  local copies, waits for them, and re-layouts: 16.4 us -> 35.3 us
    all_gather x1, waiting for transfers between devices: 58.1 us -> 18.8 us  [per_device(): full_rows = lax.all_gather(tokens, 'mp', axis=1, tiled=True)]
    unnamed x30 -> x55, local copies, waits for them, and re-layouts: 9.83 us -> 27.6 us
    unnamed x3, waiting for transfers between devices: 8.67 us -> 25.6 us
    all_to_all x1, waiting for transfers between devices: 14.6 us -> 0.01 us  [per_device(): lax.all_to_all(made[0], 'dp', split_axis=0, concat_axis=1, tiled=True)]
    all_to_all x1, starting transfers between devices: 3.84 us -> 14.2 us  [per_device(): lax.all_to_all(made[0], 'dp', split_axis=0, concat_axis=1, tiled=True)]
    all_to_all x1, starting transfers between devices: 5.21 us -> 14 us  [swap_blocks(): received = lax.all_to_all(jnp.stack(parts), axis, 0, 0)]
    all_to_all x1, waiting for transfers between devices: 5.21 us -> 0.02 us  [swap_blocks(): received = lax.all_to_all(jnp.stack(parts), axis, 0, 0)]
    all_to_all x3, waiting for transfers between devices: 41.7 us -> 37 us  [from_everyone(): return lax.all_to_all(copies, axis, split_axis=0, concat_axis=0, tiled=True)]
  transfers between devices with their start and end apart: 7 -> 7, of which waited for: 7 -> 4; matrix products, arithmetic and copies ran while one was open for 5% -> 25% of each run, Pallas kernels for 0% -> 0%
where the time goes in v1:
time: 213 us; the launch traced here: 212 us
  waiting for transfers between devices  81.4 us (38%)
  starting transfers between devices  58.5 us (27%)
  local copies, waits for them, and re-layouts  35.3 us (17%)
  matrix products  15.6 us (7%)
  between operations  14.3 us (7%)
  other arithmetic  7.06 us (3%)
    all_to_all x3, waiting for transfers between devices, from_everyone(): return lax.all_to_all(copies, axis, split_axis=0, concat_axis=0, tiled=True)  37 us
    all_to_all x3, starting transfers between devices, from_everyone(): return lax.all_to_all(copies, axis, split_axis=0, concat_axis=0, tiled=True)  30.2 us
    unnamed x55, local copies, waits for them, and re-layouts  27.6 us
    unnamed x3, waiting for transfers between devices  25.6 us
    all_gather x1, waiting for transfers between devices, per_device(): full_rows = lax.all_gather(tokens, 'mp', axis=1, tiled=True)  18.8 us
    dot_general x5, matrix products, matmul(): return jnp.dot(left, right, preferred_element_type=jnp.float32)  15 us
    all_to_all x1, starting transfers between devices, per_device(): lax.all_to_all(made[0], 'dp', split_axis=0, concat_axis=1, tiled=True)  14.2 us
    all_to_all x1, starting transfers between devices, swap_blocks(): received = lax.all_to_all(jnp.stack(parts), axis, 0, 0)  14 us
  transfers between devices with their start and end apart: 7, of which 4 were waited for; matrix products, arithmetic and copies ran while one was open for 25% of the time, Pallas kernels for 0%

profile of v1, /device:TPU:25, one launch (start us, length us, event | category | flops | bytes accessed | tf_op | source)
XLA Modules:
  0.0 212.1 jit_solution(1439686125442147526)
XLA Ops:
  6.5 0.7 all-gather.2.cloned.1.call-update
  7.3 1.3 broadcast_in_dim.38
  8.5 17.7 %all-to-all-start = ((s32[32,1,8]{2,1,0:T(1,128)}), s32[32,1,8]{2,1,0:T(1,128)S(1)}, u32[]{:S(2)}, u32[]{:S(2)}) async-start(s32[32,1,8]{2,1,0:T(1,128)} %broadcast_in_dim.38), calls=%async_computation | async-start | bytes 32768 | tf_op jit(solution)/shard_map/all_to_all | solution.py:23
  26.8 0.7 convert.7
  27.5 0.7 fusion.29
  28.3 0.8 fusion.17
  29.2 0.7 convert_element_type.45
  29.9 0.7 reshape.141
  30.6 9.2 %all-to-all-done = s32[32,1,8]{2,1,0:T(1,128)S(1)} async-done(((s32[32,1,8]{2,1,0:T(1,128)}), s32[32,1,8]{2,1,0:T(1,128)S(1)}, u32[]{:S(2)}, u32[]{:S(2)}) %all-to-all-start) | async-done | bytes 1056 | tf_op jit(solution)/shard_map/all_to_all | solution.py:23
  39.8 6.4 %all-to-all-start.1 = ((bf16[16,2,256]{2,1,0:T(2,128)(2,1)}), bf16[16,2,256]{2,1,0:T(2,128)(2,1)S(1)}, u32[]{:S(2)}, u32[]{:S(2)}) async-start(bf16[16,2,256]{2,1,0:T(2,128)(2,1)} %reshape.141), calls=%async_computation.1 | async-start | bytes 32768 | tf_op jit(solution)/shard_map/all_to_all | solution.py:23
  47.5 18.8 %all-gather.2.cloned.1.call-done = bf16[1024,2048]{1,0:T(8,128)(2,1)} async-done(((bf16[1024,128]{1,0:T(8,128)(2,1)}), bf16[1024,2048]{1,0:T(8,128)(2,1)}) %all-gather.2.cloned.1.call-update) | async-done | bytes 4194320 | tf_op jit(solution)/shard_map/all_gather | solution.py:70
  66.3 3.2 %fusion = f32[1024]{0:T(1024)S(1)} fusion(bf16[1024,2048]{1,0:T(8,128)(2,1)} %all-gather.2.cloned.1.call-done), kind=kLoop, calls=%fused_computation.3 | loop fusion | flops 6290432 | bytes 4198400 | tf_op jit(solution)/shard_map/reduce_sum | solution.py:72
  69.8 4.2 %fusion.12 = f32[1024,320]{0,1:T(8,128)} fusion(bf16[2048,320]{0,1:T(8,128)(2,1)} %param.14, bf16[1024,2048]{1,0:T(8,128)(2,1)S(1)} %copy-done.1, f32[2048]{0:T(1024)S(1)} %convert_element_type.45, f32[1024]{0:T(1024)S(1)} %add_rsqrt_fusion), kind=kOutput, calls=%fused_computation.18 | convolution fusion | flops 1350565888 | bytes 6828032 | tf_op jit(solution)/shard_map/dot_general | solution.py:36
  74.0 8.6 %convolution_convert_fusion = bf16[1024,2048]{1,0:T(8,128)(2,1)} fusion(bf16[320,2048]{1,0:T(8,128)(2,1)S(1)} %copy-done, bf16[2048,320]{0,1:T(8,128)(2,1)S(1)} %copy-done.7, f32[1024,320]{0,1:T(8,128)} %fusion.12, bf16[1024,2048]{1,0:T(8,128)(2,1)} %all-gather.2.cloned.1.call-done, f32[2048]{0:T(1024)S(1)} %convert_element_type.45, f32[1024]{0:T(1024)S(1)} %add_rsqrt_fusion), kind=kOutput, calls=%fused_computation.7 | convolution fusion | flops 2698117120 | bytes 12333056 | tf_op jit(solution)/shard_map/dot_general | solution.py:36
  82.6 6.4 %copy.23 = bf16[1024,2048]{0,1:T(8,128)(2,1)} copy(bf16[1024,2048]{1,0:T(8,128)(2,1)} %convolution_convert_fusion) | data formatting | bytes 8388608
  89.3 1.2 gather_fusion
  90.5 1.0 fusion.14
  91.5 14.2 %all-to-all-start.2 = ((bf16[32,8,256]{2,1,0:T(8,128)(2,1)}), bf16[32,8,256]{2,1,0:T(8,128)(2,1)S(1)}, u32[]{:S(2)}, u32[]{:S(2)}) async-start(bf16[32,8,256]{2,1,0:T(8,128)(2,1)} %fusion.14), calls=%async_computation.2 | async-start | bytes 262144 | tf_op jit(solution)/shard_map/all_to_all | solution.py:67
  106.0 0.6 constant_dynamic-update-slice_fusion.31
  106.6 0.6 constant_dynamic-update-slice_fusion.30
  107.8 0.6 constant_dynamic-update-slice_fusion.28
  108.4 0.6 constant_dynamic-update-slice_fusion.27
  125.0 14.0 %all-to-all-start.4 = ((bf16[32,8,256]{2,1,0:T(8,128)(2,1)}), bf16[32,8,256]{2,1,0:T(8,128)(2,1)S(1)}, u32[]{:S(2)}, u32[]{:S(2)}) async-start(bf16[32,8,256]{2,1,0:T(8,128)(2,1)} %constant_dynamic-update-slice_fusion), calls=%async_computation.4 | async-start | bytes 262144 | tf_op jit(solution)/shard_map/all_to_all | solution.py:11
  139.3 24.9 %reduce-scatter.4.cloned.1.call-done = bf16[128,1024]{1,0:T(8,128)(2,1)} async-done(((bf16[2048,1024]{1,0:T(8,128)(2,1)}), bf16[128,1024]{1,0:T(8,128)(2,1)}) %reduce-scatter.4.cloned.1.call-update) | async-done | bytes 262160
  164.2 1.1 copy.24
  165.6 1.9 broadcast_in_dim.46
  167.5 6.1 %all-to-all-start.3 = ((bf16[16,8,128,64]{2,3,1,0:T(8,128)(2,1)}), bf16[16,8,128,64]{2,3,1,0:T(8,128)(2,1)S(1)}, u32[]{:S(2)}, u32[]{:S(2)}) async-start(bf16[16,8,128,64]{2,3,1,0:T(8,128)(2,1)} %broadcast_in_dim.46), calls=%async_computation.3 | async-start | bytes 4194304 | tf_op jit(solution)/shard_map/all_to_all | solution.py:23
  173.6 0.9 copy.19
  174.5 0.9 reshape_reshape.3
  175.4 27.8 %all-to-all-done.3 = bf16[16,8,128,64]{2,3,1,0:T(8,128)(2,1)S(1)} async-done(((bf16[16,8,128,64]{2,3,1,0:T(8,128)(2,1)}), bf16[16,8,128,64]{2,3,1,0:T(8,128)(2,1)S(1)}, u32[]{:S(2)}, u32[]{:S(2)}) %all-to-all-start.3) | async-done | bytes 2097184 | tf_op jit(solution)/shard_map/all_to_all | solution.py:23
  203.5 0.6 copy-done.5
  204.4 0.8 fusion.22
  (72 shorter events, 20.0 us)
Async XLA Ops:
  6.5 67.4 %copy-start = (bf16[320,2048]{1,0:T(8,128)(2,1)S(1)}, bf16[320,2048]{1,0:T(8,128)(2,1)}, u32[]{:S(2)}) copy-start(bf16[320,2048]{1,0:T(8,128)(2,1)} %param.16) | copy-start | bytes 3932164
  6.5 59.8 %all-gather.2.cloned.1.call-start = ((), (), s32[]{:S(2)}) async-start(), calls=%async_computation.6 | async-start | bytes 4456448 | tf_op jit(solution)/shard_map/all_gather | solution.py:70
  8.5 31.2 %all-to-all-start = ((s32[32,1,8]{2,1,0:T(1,128)}), s32[32,1,8]{2,1,0:T(1,128)S(1)}, u32[]{:S(2)}, u32[]{:S(2)}) async-start(s32[32,1,8]{2,1,0:T(1,128)} %broadcast_in_dim.38), calls=%async_computation | async-start | bytes 32768 | tf_op jit(solution)/shard_map/all_to_all | solution.py:23
  39.8 49.3 %all-to-all-start.1 = ((bf16[16,2,256]{2,1,0:T(2,128)(2,1)}), bf16[16,2,256]{2,1,0:T(2,128)(2,1)S(1)}, u32[]{:S(2)}, u32[]{:S(2)}) async-start(bf16[16,2,256]{2,1,0:T(2,128)(2,1)} %reshape.141), calls=%async_computation.1 | async-start | bytes 32768 | tf_op jit(solution)/shard_map/all_to_all | solution.py:23
  46.2 117.9 %reduce-scatter.4.cloned.1.call-start = ((), (), s32[]{:S(2)}) async-start(), calls=%async_computation.7 | async-start | bytes 4456448
  66.3 3.4 %copy-start.1 = (bf16[1024,2048]{1,0:T(8,128)(2,1)S(1)}, bf16[1024,2048]{1,0:T(8,128)(2,1)}, u32[]{:S(2)}) copy-start(bf16[1024,2048]{1,0:T(8,128)(2,1)} %all-gather.2.cloned.1.call-done) | copy-start | bytes 12582916
  69.8 4.2 %copy-start.7 = (bf16[2048,320]{0,1:T(8,128)(2,1)S(1)}, bf16[2048,320]{0,1:T(8,128)(2,1)}, u32[]{:S(2)}) copy-start(bf16[2048,320]{0,1:T(8,128)(2,1)} %param.15) | copy-start | bytes 3932164
  89.3 1.2 copy-start.8
  90.5 15.2 %copy-start.9 = (bf16[1024,256]{1,0:T(8,128)(2,1)S(1)}, bf16[1024,256]{1,0:T(8,128)(2,1)}, u32[]{:S(2)}) copy-start(bf16[1024,256]{1,0:T(8,128)(2,1)} %param.23) | copy-start | bytes 1572868
  91.5 33.6 %all-to-all-start.2 = ((bf16[32,8,256]{2,1,0:T(8,128)(2,1)}), bf16[32,8,256]{2,1,0:T(8,128)(2,1)S(1)}, u32[]{:S(2)}, u32[]{:S(2)}) async-start(bf16[32,8,256]{2,1,0:T(8,128)(2,1)} %fusion.14), calls=%async_computation.2 | async-start | bytes 262144 | tf_op jit(solution)/shard_map/all_to_all | solution.py:67
  125.0 40.6 %all-to-all-start.4 = ((bf16[32,8,256]{2,1,0:T(8,128)(2,1)}), bf16[32,8,256]{2,1,0:T(8,128)(2,1)S(1)}, u32[]{:S(2)}, u32[]{:S(2)}) async-start(bf16[32,8,256]{2,1,0:T(8,128)(2,1)} %constant_dynamic-update-slice_fusion), calls=%async_computation.4 | async-start | bytes 262144 | tf_op jit(solution)/shard_map/all_to_all | solution.py:11
  165.3 2.2 %copy-start.2 = (bf16[1024,128]{1,0:T(8,128)(2,1)}, bf16[1024,128]{1,0:T(8,128)(2,1)S(1)}, u32[]{:S(2)}) copy-start(bf16[1024,128]{1,0:T(8,128)(2,1)S(1)} %copy.24) | copy-start | bytes 786436
  165.6 1.9 copy-start.6
  167.5 35.7 %all-to-all-start.3 = ((bf16[16,8,128,64]{2,3,1,0:T(8,128)(2,1)}), bf16[16,8,128,64]{2,3,1,0:T(8,128)(2,1)S(1)}, u32[]{:S(2)}, u32[]{:S(2)}) async-start(bf16[16,8,128,64]{2,3,1,0:T(8,128)(2,1)} %broadcast_in_dim.46), calls=%async_computation.3 | async-start | bytes 4194304 | tf_op jit(solution)/shard_map/all_to_all | solution.py:23
  203.2 1.0 copy-start.5
  203.2 1.3 copy-start.3
  203.2 1.3 copy-start.4
Sparse Core Ops, SparseCore 0:
  9.4 56.8 all-gather.1
  89.1 74.9 reduce-scatter.3
